TPU v7x, 512 devices: a whole 4x8x8 slice. The times are simulated.
512 devices in a mesh: dp: 16 (over y, z_lo), fsdp: 32 (over x, z_hi, core).
Axes of the slice: x: 4, y: 8, z: 8 (z_hi: 4, z_lo: 2; z = z_hi * 2 + z_lo), core: 2. Of those that a mesh axis runs over, the one named last changes fastest.
Arguments:
- signal: bfloat16 [131072, 1024], P(('dp', 'fsdp')), may hold values from -6 to 6
- grad_gated: bfloat16 [131072, 512], P(('dp', 'fsdp')), may hold values from -24 to 24
- conv_weight: bfloat16 [1024, 3072], P('fsdp'), may hold values from -0.109375 to 0.109375
- source_seg: int32 [512, 32], P(('dp', 'fsdp')), may hold values from -1 to 1023, as said below
Outputs:
- gated_out: bfloat16 [131072, 512], P(('dp', 'fsdp'))
- grad_in: bfloat16 [131072, 1024], P(('dp', 'fsdp'))
- grad_weight: float32 [1024, 3072], P('fsdp')
Inputs may be any that keep to these rules, and one draw needn't show every extreme that they name: `source_seg`: -1 where a stream begins. The preceding segment holds the same position on its device as g on its own, no two segments of one device take their left context from the same device, and every segment precedes at most one segment.
All inputs are finite; a program needn't handle non-finite values.
Results may differ from a plain program's by a relative error of at most 0.0049.
Values may be sent and summed in bfloat16 or wider, within the bound.
A program may use at most 64 MiB of HBM per device.

v0:
```python
import math
import jax
import jax.numpy as jnp
from jax import lax
from jax.sharding import PartitionSpec as P

C = 1024
H = 512
DILATION_SIZE = 4


def tap_starts(context_row_block):
    return [context_row_block - (2 - selected_index) * DILATION_SIZE for selected_index in range(3)]


def per_device(signal, grad_gated, conv_weight, source_seg):
    peer_count = lax.axis_size("fsdp")
    seg_count = source_seg.shape[1]
    row_count = signal.shape[0]
    seg_rows = row_count // seg_count
    context_row_block = 2 * DILATION_SIZE
    starts = tap_starts(context_row_block)
    segments = signal.reshape(seg_count, seg_rows, C)
    sources = source_seg[0]
    source_dev = jnp.where(sources >= 0, sources // seg_count, -1)
    peers = jnp.arange(peer_count, dtype=jnp.int32)
    request_mask = (source_dev[None, :] == peers[:, None]).astype(jnp.int32)
    asked = lax.all_to_all(request_mask, "fsdp", split_axis=0, concat_axis=0, tiled=True)
    send_table = asked.astype(jnp.bfloat16)
    recv_table = (source_dev[:, None] == peers[None, :]).astype(jnp.bfloat16)
    outgoing = jnp.einsum(
        "ns,slc->nlc", send_table, segments, preferred_element_type=jnp.float32
    ).astype(jnp.bfloat16)
    incoming = lax.all_to_all(outgoing, "fsdp", split_axis=0, concat_axis=0, tiled=True)
    carries = jnp.einsum(
        "sn,nlc->slc", recv_table, incoming, preferred_element_type=jnp.float32
    ).astype(jnp.bfloat16)
    extended = jnp.concatenate([carries, segments], axis=1)
    full_weight = lax.all_gather(conv_weight, "fsdp", axis=0, tiled=True)
    contract_final_axis = (((1,), (1,)), ((), ()))
    contract_first = (((0,), (0,)), ((), ()))
    windows = [extended[:, start : start + seg_rows, :].reshape(row_count, C) for start in starts]
    preact = sum(
        (
            lax.dot_general(
                windows[selected_index],
                full_weight[:, selected_index * C : (selected_index + 1) * C],
                contract_final_axis,
                preferred_element_type=jnp.float32,
            )
            for selected_index in range(3)
        )
    )
    filter_act = jnp.tanh(preact[:, :H])
    gate_act = jax.nn.sigmoid(preact[:, H:])
    gated_out = (filter_act * gate_act).astype(jnp.bfloat16)
    upstream_wide = grad_gated.astype(jnp.float32)
    grad_pre = jnp.concatenate(
        [
            upstream_wide * gate_act * (1.0 - filter_act * filter_act),
            upstream_wide * filter_act * gate_act * (1.0 - gate_act),
        ],
        axis=1,
    ).astype(jnp.bfloat16)
    partial_value = jnp.concatenate(
        [
            lax.dot_general(
                grad_pre,
                windows[selected_index],
                contract_first,
                preferred_element_type=jnp.float32,
            ).astype(jnp.bfloat16)
            for selected_index in range(3)
        ],
        axis=1,
    )
    arrived = lax.all_to_all(partial_value, "fsdp", split_axis=0, concat_axis=0, tiled=True)
    shard_sum = jnp.sum(arrived.reshape(peer_count, -1, 3 * C), axis=0, dtype=jnp.float32)
    group_total = lax.psum(shard_sum, "dp")
    total_token_count = row_count * peer_count * lax.axis_size("dp")
    grad_weight = group_total * (1.0 / math.sqrt(total_token_count))
    back_proj = jnp.dot(grad_pre, full_weight, preferred_element_type=jnp.float32)
    back_proj = back_proj.reshape(seg_count, seg_rows, 3 * C)
    grad_ext = jnp.zeros((seg_count, context_row_block + seg_rows, C), jnp.float32)
    for selected_index, start in enumerate(starts):
        grad_ext = grad_ext.at[:, start : start + seg_rows, :].add(
            back_proj[:, :, selected_index * C : (selected_index + 1) * C]
        )
    outgoing_grad = jnp.einsum(
        "sn,slc->nlc",
        recv_table.astype(jnp.float32),
        grad_ext[:, :context_row_block, :],
        precision=lax.Precision.HIGHEST,
    )
    incoming_grad = lax.all_to_all(outgoing_grad, "fsdp", split_axis=0, concat_axis=0, tiled=True)
    tail_grad = jnp.einsum(
        "ns,nlc->slc",
        send_table.astype(jnp.float32),
        incoming_grad,
        precision=lax.Precision.HIGHEST,
    )
    grad_in = (
        grad_ext[:, context_row_block:, :].at[:, seg_rows - context_row_block :, :].add(tail_grad)
    )
    grad_in = grad_in.reshape(row_count, C).astype(jnp.bfloat16)
    return (gated_out, grad_in, grad_weight)


def solution(mesh):
    placed = (
        P(("dp", "fsdp"), None),
        P(("dp", "fsdp"), None),
        P("fsdp", None),
        P(("dp", "fsdp"), None),
    )
    return jax.shard_map(
        per_device,
        mesh=mesh,
        in_specs=placed,
        out_specs=(P(("dp", "fsdp"), None), P(("dp", "fsdp"), None), P("fsdp", None)),
        check_vma=False,
    )
```

profile of v0, /device:TPU:2, one launch (start us, length us, event | category | flops | bytes accessed | tf_op | source)
XLA Modules:
  0.0 440.9 jit_solution(733692016285793341)
XLA Ops:
  8.6 21.8 %all_to_all.25 = s32[32,1,32]{2,1,0:T(1,128)S(1)} all-to-all(s32[32,1,32]{2,1,0:T(1,128)S(1)} %compare_convert_fusion), channel_id=1, replica_groups=mesh['dp'=16,'fsdp'=32] {'fsdp'}, dimensions={0} | all-to-all | bytes 8192 | tf_op jit(solution)/shard_map/all_to_all | solution.py:28
  30.4 1.8 convolution_convert_fusion.4
  32.3 1.1 copy.20
  33.4 5.0 %all-to-all-start.1 = ((bf16[32,8,1024]{2,1,0:T(8,128)(2,1)}), bf16[32,8,1024]{2,1,0:T(8,128)(2,1)S(1)}, u32[]{:S(2)}, u32[]{:S(2)}) async-start(bf16[32,8,1024]{2,1,0:T(8,128)(2,1)} %copy.20), calls=%async_computation.1 | async-start | bytes 1048576 | tf_op jit(solution)/shard_map/all_to_all | solution.py:34
  38.4 1.3 copy.19
  39.8 17.5 %all-to-all-done.1 = bf16[32,8,1024]{2,1,0:T(8,128)(2,1)S(1)} async-done(((bf16[32,8,1024]{2,1,0:T(8,128)(2,1)}), bf16[32,8,1024]{2,1,0:T(8,128)(2,1)S(1)}, u32[]{:S(2)}, u32[]{:S(2)}) %all-to-all-start.1) | async-done | bytes 524320 | tf_op jit(solution)/shard_map/all_to_all | solution.py:34
  58.1 39.0 %all-gather.2.cloned.1.call-done = bf16[1024,3072]{1,0:T(8,128)(2,1)} async-done(((bf16[32,3072]{1,0:T(8,128)(2,1)}), bf16[1024,3072]{1,0:T(8,128)(2,1)}) %all-gather.2.cloned.1.call-update) | async-done | bytes 6291472 | tf_op jit(solution)/shard_map/all_gather | solution.py:39
  97.1 2.3 fusion
  99.4 2.5 fusion.2
  101.9 2.5 fusion.9
  107.9 13.4 %pad_maximum_fusion = bf16[1024,3072]{0,1:T(8,128)(2,1)} fusion(bf16[1024,1024]{0,1:T(8,128)(2,1)S(1)} %convolution_convert_fusion, bf16[1024,1024]{0,1:T(8,128)(2,1)S(1)} %convolution_convert_fusion.1, bf16[1024,1024]{0,1:T(8,128)(2,1)S(1)} %convolution_convert_fusion.2), kind=kLoop, calls=%fused_computation.1 | loop fusion | flops 18874368 | bytes 12582912 | tf_op jit(solution)/shard_map/concatenate | solution.py:65
  121.3 8.6 %copy.33 = bf16[1024,3072]{1,0:T(8,128)(2,1)} copy(bf16[1024,3072]{0,1:T(8,128)(2,1)} %pad_maximum_fusion) | data formatting | bytes 12582912 | tf_op jit(solution)/shard_map/concatenate | solution.py:65
  129.9 6.8 %all-to-all-start.3 = ((bf16[32,32,3072]{2,1,0:T(8,128)(2,1)}), bf16[32,32,3072]{2,1,0:T(8,128)(2,1)}, u32[]{:S(2)}, u32[]{:S(2)}) async-start(bf16[32,32,3072]{2,1,0:T(8,128)(2,1)} %bitcast.44), calls=%async_computation.3 | async-start | bytes 12582912 | tf_op jit(solution)/shard_map/all_to_all | solution.py:77
  136.7 4.6 %convolution_bitcast_fusion = f32[32,8,3072]{2,1,0:T(8,128)S(1)} fusion(bf16[1024,3072]{1,0:T(8,128)(2,1)} %all-gather.2.cloned.1.call-done, bf16[256,512]{1,0:T(8,128)(2,1)S(1)} %get-tuple-element.63, bf16[256,512]{1,0:T(8,128)(2,1)S(1)} %get-tuple-element.62), kind=kOutput, calls=%fused_computation.2 | convolution fusion | flops 1611661312 | bytes 9961472 | tf_op jit(solution)/shard_map/dot_general | solution.py:82
  141.3 1.4 fusion.45
  145.2 1.6 copy.29
  146.7 130.2 %all-to-all-done.3 = bf16[32,32,3072]{2,1,0:T(8,128)(2,1)} async-done(((bf16[32,32,3072]{2,1,0:T(8,128)(2,1)}), bf16[32,32,3072]{2,1,0:T(8,128)(2,1)}, u32[]{:S(2)}, u32[]{:S(2)}) %all-to-all-start.3) | async-done | bytes 6291488 | tf_op jit(solution)/shard_map/all_to_all | solution.py:77
  277.0 8.6 %all-to-all-start.2 = ((f32[32,8,1024]{2,1,0:T(8,128)}), f32[32,8,1024]{2,1,0:T(8,128)S(1)}, u32[]{:S(2)}, u32[]{:S(2)}) async-start(f32[32,8,1024]{2,1,0:T(8,128)} %copy.29), calls=%async_computation.2 | async-start | bytes 2097152 | tf_op jit(solution)/shard_map/all_to_all | solution.py:95
  285.6 4.8 %convert_reduce_fusion = f32[32,3072]{1,0:T(8,128)} fusion(bf16[32,32,3072]{2,1,0:T(8,128)(2,1)} %all-to-all-done.3), kind=kLoop, calls=%fused_computation | loop fusion | flops 6193152 | bytes 6684672 | tf_op jit(solution)/shard_map/reduce_sum | solution.py:78
  290.5 20.6 %all-to-all-done.2 = f32[32,8,1024]{2,1,0:T(8,128)S(1)} async-done(((f32[32,8,1024]{2,1,0:T(8,128)}), f32[32,8,1024]{2,1,0:T(8,128)S(1)}, u32[]{:S(2)}, u32[]{:S(2)}) %all-to-all-start.2) | async-done | bytes 1048608 | tf_op jit(solution)/shard_map/all_to_all | solution.py:95
  311.1 3.0 fusion.12
  314.1 1.1 copy.68
  315.2 117.1 %all-reduce.3.cloned.1.call-done = f32[32,3072]{1,0:T(8,128)} async-done(((f32[32,3072]{1,0:T(8,128)}), f32[32,3072]{1,0:T(8,128)}) %all-reduce.3.cloned.1.call-update) | async-done | bytes 393232 | tf_op jit(solution)/shard_map/psum | solution.py:79
  432.3 1.8 broadcast_multiply_fusion
  (23 shorter events, 8.2 us)
Async XLA Ops:
  7.2 32.6 %copy-start.2 = (s32[1,32]{1,0:T(1,128)S(1)}, s32[1,32]{1,0:T(1,128)}, u32[]{:S(2)}) copy-start(s32[1,32]{1,0:T(1,128)} %param.17) | copy-start | bytes 388
  7.2 89.9 %copy-start = (bf16[256,1024]{1,0:T(8,128)(2,1)S(1)}, bf16[256,1024]{1,0:T(8,128)(2,1)}, u32[]{:S(2)}) copy-start(bf16[256,1024]{1,0:T(8,128)(2,1)} %param.14) | copy-start | bytes 1572868
  7.2 89.9 %all-gather.2.cloned.1.call-start = ((), (), s32[]{:S(2)}) async-start(), calls=%async_computation.4 | async-start | bytes 6488064 | tf_op jit(solution)/shard_map/all_gather | solution.py:39
  33.4 23.9 %all-to-all-start.1 = ((bf16[32,8,1024]{2,1,0:T(8,128)(2,1)}), bf16[32,8,1024]{2,1,0:T(8,128)(2,1)S(1)}, u32[]{:S(2)}, u32[]{:S(2)}) async-start(bf16[32,8,1024]{2,1,0:T(8,128)(2,1)} %copy.20), calls=%async_computation.1 | async-start | bytes 1048576 | tf_op jit(solution)/shard_map/all_to_all | solution.py:34
  99.4 5.0 %copy-start.1 = (bf16[256,512]{1,0:T(8,128)(2,1)S(1)}, bf16[256,512]{1,0:T(8,128)(2,1)}, u32[]{:S(2)}) copy-start(bf16[256,512]{1,0:T(8,128)(2,1)} %param.15) | copy-start | bytes 786436
  129.9 147.1 %all-to-all-start.3 = ((bf16[32,32,3072]{2,1,0:T(8,128)(2,1)}), bf16[32,32,3072]{2,1,0:T(8,128)(2,1)}, u32[]{:S(2)}, u32[]{:S(2)}) async-start(bf16[32,32,3072]{2,1,0:T(8,128)(2,1)} %bitcast.44), calls=%async_computation.3 | async-start | bytes 12582912 | tf_op jit(solution)/shard_map/all_to_all | solution.py:77
  277.0 34.1 %all-to-all-start.2 = ((f32[32,8,1024]{2,1,0:T(8,128)}), f32[32,8,1024]{2,1,0:T(8,128)S(1)}, u32[]{:S(2)}, u32[]{:S(2)}) async-start(f32[32,8,1024]{2,1,0:T(8,128)} %copy.29), calls=%async_computation.2 | async-start | bytes 2097152 | tf_op jit(solution)/shard_map/all_to_all | solution.py:95
  285.6 146.7 %all-reduce.3.cloned.1.call-start = ((), (), s32[]{:S(2)}) async-start(), calls=%async_computation.5 | async-start | bytes 786432 | tf_op jit(solution)/shard_map/psum | solution.py:79
Sparse Core Ops, SparseCore 0:
  11.1 85.8 all-gather.1
  290.6 141.6 all-reduce.2
where the time goes:
time: 442 us; the launch traced here: 441 us
  waiting for transfers between devices  325 us (74%)
  other arithmetic  22.7 us (5%)
  blocking collectives  21.8 us (5%)
  starting transfers between devices  20.5 us (5%)
  matrix products  20.5 us (5%)
  local copies, waits for them, and re-layouts  16 us (4%)
  between operations  14.2 us (3%)
    all_to_all x1, waiting for transfers between devices, per_device(): lax.all_to_all(partial_value, 'fsdp', split_axis=0, concat_axis=0, tiled=...  130 us
    psum x1, waiting for transfers between devices, per_device(): group_total = lax.psum(shard_sum, 'dp')  117 us
    all_gather x1, waiting for transfers between devices, per_device(): full_weight = lax.all_gather(conv_weight, 'fsdp', axis=0, tiled=True)  39 us
    all_to_all x1, blocking collectives, per_device(): lax.all_to_all(request_mask, 'fsdp', split_axis=0, concat_axis=0, tiled=T...  21.8 us
    all_to_all x1, waiting for transfers between devices, per_device(): lax.all_to_all(outgoing_grad, 'fsdp', split_axis=0, concat_axis=0, tiled=...  20.6 us
    all_to_all x1, waiting for transfers between devices, per_device(): lax.all_to_all(outgoing, 'fsdp', split_axis=0, concat_axis=0, tiled=True)  17.5 us
    concatenate x1, other arithmetic, per_device(): jnp.concatenate([lax.dot_general(grad_pre, windows[selected_index], contr...  13.4 us
  transfers between devices with their start and end apart: 5, of which 5 were waited for; matrix products, arithmetic and copies ran while one was open for 6% of the time, Pallas kernels for 0%

commit v1 on v0

--- a/solution.py
+++ b/solution.py
@@ -3,6 +3,7 @@
 import jax.numpy as jnp
 from jax import lax
 from jax.sharding import PartitionSpec as P
+from jax.lax import all_gather
 
 C = 1024
 H = 512
@@ -76,7 +77,7 @@
     )
     arrived = lax.all_to_all(partial_value, "fsdp", split_axis=0, concat_axis=0, tiled=True)
     shard_sum = jnp.sum(arrived.reshape(peer_count, -1, 3 * C), axis=0, dtype=jnp.float32)
-    group_total = lax.psum(shard_sum, "dp")
+    group_total = all_gather(shard_sum, "dp").sum(axis=0)
     total_token_count = row_count * peer_count * lax.axis_size("dp")
     grad_weight = group_total * (1.0 / math.sqrt(total_token_count))
     back_proj = jnp.dot(grad_pre, full_weight, preferred_element_type=jnp.float32)

time: 442 us -> 456 us (1.032)
  the two profiles are of different devices: /device:TPU:2 before, /device:TPU:27 now
where the time goes in v1:
time: 456 us; the launch traced here: 455 us
  blocking collectives  227 us (50%)
  waiting for transfers between devices  153 us (34%)
  other arithmetic  22 us (5%)
  matrix products  19.3 us (4%)
  between operations  14.2 us (3%)
  local copies, waits for them, and re-layouts  14 us (3%)
  starting transfers between devices  5.29 us (1%)
    all_to_all x1, blocking collectives, per_device(): lax.all_to_all(partial_value, 'fsdp', split_axis=0, concat_axis=0, tiled=...  148 us
    all_gather x1, waiting for transfers between devices, per_device(): group_total = all_gather(shard_sum, 'dp').sum(axis=0)  96.1 us
    all_to_all x1, blocking collectives, per_device(): lax.all_to_all(outgoing_grad, 'fsdp', split_axis=0, concat_axis=0, tiled=...  57.8 us
    all_gather x1, waiting for transfers between devices, per_device(): full_weight = lax.all_gather(conv_weight, 'fsdp', axis=0, tiled=True)  39.4 us
    all_to_all x1, blocking collectives, per_device(): lax.all_to_all(request_mask, 'fsdp', split_axis=0, concat_axis=0, tiled=T...  21.9 us
    all_to_all x1, waiting for transfers between devices, per_device(): lax.all_to_all(outgoing, 'fsdp', split_axis=0, concat_axis=0, tiled=True)  16.9 us
    concatenate x1, other arithmetic, per_device(): jnp.concatenate([lax.dot_general(grad_pre, windows[selected_index], contr...  13.4 us
  transfers between devices with their start and end apart: 3, of which 3 were waited for; matrix products, arithmetic and copies ran while one was open for 4% of the time, Pallas kernels for 0%

profile of v1, /device:TPU:27, one launch (start us, length us, event | category | flops | bytes accessed | tf_op | source)
XLA Modules:
  0.0 455.1 jit_solution(9515092726578908465)
XLA Ops:
  8.6 21.9 %all_to_all.25 = s32[32,1,32]{2,1,0:T(1,128)S(1)} all-to-all(s32[32,1,32]{2,1,0:T(1,128)S(1)} %compare_convert_fusion), channel_id=1, replica_groups=mesh['dp'=16,'fsdp'=32] {'fsdp'}, dimensions={0} | all-to-all | bytes 8192 | tf_op jit(solution)/shard_map/all_to_all | solution.py:29
  30.6 1.8 convolution_convert_fusion.4
  32.4 1.1 copy.36
  33.5 5.2 %all-to-all-start.1 = ((bf16[32,8,1024]{2,1,0:T(8,128)(2,1)}), bf16[32,8,1024]{2,1,0:T(8,128)(2,1)S(1)}, u32[]{:S(2)}, u32[]{:S(2)}) async-start(bf16[32,8,1024]{2,1,0:T(8,128)(2,1)} %copy.36), calls=%async_computation.1 | async-start | bytes 1048576 | tf_op jit(solution)/shard_map/all_to_all | solution.py:35
  38.8 1.3 copy.35
  40.1 16.9 %all-to-all-done.1 = bf16[32,8,1024]{2,1,0:T(8,128)(2,1)S(1)} async-done(((bf16[32,8,1024]{2,1,0:T(8,128)(2,1)}), bf16[32,8,1024]{2,1,0:T(8,128)(2,1)S(1)}, u32[]{:S(2)}, u32[]{:S(2)}) %all-to-all-start.1) | async-done | bytes 524320 | tf_op jit(solution)/shard_map/all_to_all | solution.py:35
  57.9 39.4 %all-gather.4.cloned.1.call-done = bf16[1024,3072]{1,0:T(8,128)(2,1)} async-done(((bf16[32,3072]{1,0:T(8,128)(2,1)}), bf16[1024,3072]{1,0:T(8,128)(2,1)}) %all-gather.4.cloned.1.call-update) | async-done | bytes 6291472 | tf_op jit(solution)/shard_map/all_gather | solution.py:40
  97.2 2.3 fusion
  99.6 2.5 fusion.2
  102.1 2.5 fusion.9
  104.6 1.0 fusion.18
  105.6 0.8 convolution_convert_fusion.2
  106.4 0.8 convolution_convert_fusion.1
  108.1 13.4 %pad_maximum_fusion = bf16[1024,3072]{0,1:T(8,128)(2,1)} fusion(bf16[1024,1024]{0,1:T(8,128)(2,1)S(1)} %convolution_convert_fusion, bf16[1024,1024]{0,1:T(8,128)(2,1)S(1)} %convolution_convert_fusion.1, bf16[1024,1024]{0,1:T(8,128)(2,1)S(1)} %convolution_convert_fusion.2), kind=kLoop, calls=%fused_computation.1 | loop fusion | flops 18874368 | bytes 12582912 | tf_op jit(solution)/shard_map/concatenate | solution.py:66
  121.4 8.6 %copy.49 = bf16[1024,3072]{1,0:T(8,128)(2,1)} copy(bf16[1024,3072]{0,1:T(8,128)(2,1)} %pad_maximum_fusion) | data formatting | bytes 12582912 | tf_op jit(solution)/shard_map/concatenate | solution.py:66
  130.1 147.5 %all_to_all.26 = bf16[32,32,3072]{2,1,0:T(8,128)(2,1)S(1)} all-to-all(bf16[32,32,3072]{2,1,0:T(8,128)(2,1)} %bitcast.45), channel_id=1, replica_groups=mesh['dp'=16,'fsdp'=32] {'fsdp'}, dimensions={0} | all-to-all | bytes 12582912 | tf_op jit(solution)/shard_map/all_to_all | solution.py:78
  277.6 2.0 convert_reduce_fusion
  279.6 4.6 %convolution_bitcast_fusion = f32[32,8,3072]{2,1,0:T(8,128)S(1)} fusion(bf16[1024,3072]{1,0:T(8,128)(2,1)} %all-gather.4.cloned.1.call-done, bf16[256,512]{1,0:T(8,128)(2,1)S(1)} %get-tuple-element.63, bf16[256,512]{1,0:T(8,128)(2,1)S(1)} %get-tuple-element.62), kind=kOutput, calls=%fused_computation.2 | convolution fusion | flops 1611661312 | bytes 9961472 | tf_op jit(solution)/shard_map/dot_general | solution.py:83
  285.4 1.0 fusion.15
  287.6 57.8 %all_to_all.27 = f32[32,8,1024]{2,1,0:T(8,128)S(1)} all-to-all(f32[32,8,1024]{2,1,0:T(8,128)S(1)} %copy.45), channel_id=1, replica_groups=mesh['dp'=16,'fsdp'=32] {'fsdp'}, dimensions={0} | all-to-all | bytes 2097152 | tf_op jit(solution)/shard_map/all_to_all | solution.py:96
  345.4 1.8 fusion.12
  347.2 1.1 copy.84
  348.3 96.1 %all-gather.6.cloned.1.call-done = f32[512,3072]{1,0:T(8,128)} async-done(((f32[32,3072]{1,0:T(8,128)}), f32[512,3072]{1,0:T(8,128)}) %all-gather.6.cloned.1.call-update) | async-done | bytes 6291472 | tf_op jit(solution)/shard_map/all_gather | solution.py:80
  444.4 3.1 reduce_sum.19
  (22 shorter events, 6.2 us)
Async XLA Ops:
  7.2 32.9 %copy-start.2 = (s32[1,32]{1,0:T(1,128)S(1)}, s32[1,32]{1,0:T(1,128)}, u32[]{:S(2)}) copy-start(s32[1,32]{1,0:T(1,128)} %param.17) | copy-start | bytes 388
  7.2 90.1 %copy-start = (bf16[256,1024]{1,0:T(8,128)(2,1)S(1)}, bf16[256,1024]{1,0:T(8,128)(2,1)}, u32[]{:S(2)}) copy-start(bf16[256,1024]{1,0:T(8,128)(2,1)} %param.14) | copy-start | bytes 1572868
  7.2 90.1 %all-gather.4.cloned.1.call-start = ((), (), s32[]{:S(2)}) async-start(), calls=%async_computation.4 | async-start | bytes 6488064 | tf_op jit(solution)/shard_map/all_gather | solution.py:40
  33.5 23.6 %all-to-all-start.1 = ((bf16[32,8,1024]{2,1,0:T(8,128)(2,1)}), bf16[32,8,1024]{2,1,0:T(8,128)(2,1)S(1)}, u32[]{:S(2)}, u32[]{:S(2)}) async-start(bf16[32,8,1024]{2,1,0:T(8,128)(2,1)} %copy.36), calls=%async_computation.1 | async-start | bytes 1048576 | tf_op jit(solution)/shard_map/all_to_all | solution.py:35
  38.7 405.7 %all-gather.6.cloned.1.call-start = ((), (), s32[]{:S(2)}) async-start(), calls=%async_computation.5 | async-start | bytes 6684672 | tf_op jit(solution)/shard_map/all_gather | solution.py:80
  99.6 5.0 %copy-start.1 = (bf16[256,512]{1,0:T(8,128)(2,1)S(1)}, bf16[256,512]{1,0:T(8,128)(2,1)}, u32[]{:S(2)}) copy-start(bf16[256,512]{1,0:T(8,128)(2,1)} %param.15) | copy-start | bytes 786436
Sparse Core Ops, SparseCore 0:
  11.1 86.0 all-gather.3
  279.7 164.6 all-gather.5
